TPU v7x, 32 devices: a whole 2x2x4 slice. The times are simulated.
32 devices in a mesh: groups: 2 (over y), ctx: 16 (over z, x, core).
Axes of the slice: x: 2, y: 2, z: 4, core: 2. Of those that a mesh axis runs over, the one named last changes fastest.
Arguments:
- outer_gate: bfloat16 [32768, 256], P(('groups', 'ctx')), parts along dimension 0, may hold values from -6 to 6
- inner_gate: bfloat16 [32768, 256], P(('groups', 'ctx')), parts along dimension 0, may hold values from -6 to 6
- values: bfloat16 [32768, 256], P(('groups', 'ctx')), parts along dimension 0, may hold values from -6 to 6
- cotangent: bfloat16 [32768, 256], P(('groups', 'ctx')), parts along dimension 0, may hold values from -6 to 6
- residue: float32 [256, 16], replicated, may hold values from -0.5 to 0.5
- decay_rate: float32 [256, 16], replicated, may hold values from 1.8310547e-05 to 0.1
- skip_gain: float32 [256], replicated, may hold values from -4 to 4
Outputs:
- layer_out: bfloat16 [32768, 256], P(('groups', 'ctx')), parts along dimension 0
- grad_outer: bfloat16 [32768, 256], P(('groups', 'ctx')), parts along dimension 0
- grad_inner: bfloat16 [32768, 256], P(('groups', 'ctx')), parts along dimension 0
- grad_values: bfloat16 [32768, 256], P(('groups', 'ctx')), parts along dimension 0
There are 2 independent parts, one for each index of `groups`. A program takes and returns all parts, laid end to end along the dimension named above; an argument that names none is the same for every part. Nothing has to cross between parts.
All inputs are finite; a program needn't handle non-finite values.
Results may differ from a plain program's by a relative error of at most 0.005.
Values sent between devices are 32-bit elements; how exact they have to be, the bound alone decides.
No kernel may reach another device: no remote copies, remote signals or barrier semaphores. Data moves between devices by JAX's collectives and lax.ppermute only.
A program may use at most 128 MiB of HBM per device.

v0:
```python
import jax
import jax.numpy as jnp
from jax import lax
from jax.sharding import PartitionSpec as P


def product(pattern, first, second):
    return jnp.einsum(pattern, first, second, precision=lax.Precision.HIGH)


def shards(outer_gate, inner_gate, values, cotangent, residue, decay_rate, skip_gain):
    row_count, channels = values.shape
    block_width = min(64, row_count)
    block_count = row_count // block_width
    position = lax.axis_index("ctx")
    rate_table = decay_rate.T
    pole_weight = residue.T
    mixed_input = (inner_gate.astype(jnp.float32) * values.astype(jnp.float32)).astype(jnp.bfloat16)
    mixed_float = lax.optimization_barrier(mixed_input).astype(jnp.float32)
    offsets = jnp.arange(block_width, dtype=jnp.float32)
    enter_table = jnp.exp(-rate_table[None] * (offsets + 1.0)[:, None, None])
    leave_table = jnp.exp(-rate_table[None] * (block_width - 1.0 - offsets)[:, None, None])
    sections = jnp.arange(block_count, dtype=jnp.float32)
    powers = jnp.exp(-rate_table[None] * (block_width * sections)[:, None, None])
    reverse_powers = powers[::-1]
    later_index = jnp.arange(block_count)[:, None]
    earlier_index = jnp.arange(block_count)[None, :]
    spacing = jnp.maximum(later_index - earlier_index - 1, 0).astype(jnp.float32)
    decayed = jnp.exp(-rate_table[None, None] * (block_width * spacing)[:, :, None, None])
    carry_table = jnp.where((earlier_index < later_index)[:, :, None, None], decayed, 0.0)
    tap_values = jnp.sum(
        pole_weight[None] * jnp.exp(-rate_table[None] * offsets[:, None, None]), axis=1
    )
    differ = jnp.arange(block_width)[:, None] - jnp.arange(block_width)[None, :]
    lag_onehot = (differ[:, :, None] == jnp.arange(block_width)[None, None, :]).astype(jnp.float32)
    kernel = jnp.einsum("tsl,lc->tsc", lag_onehot, tap_values, precision=lax.Precision.HIGHEST)
    pieces = mixed_float.reshape(block_count, block_width, channels)
    span_states = product("nsc,skc->nkc", pieces, leave_table)
    own_state = jnp.sum(span_states * reverse_powers, axis=0)
    within = product("nsc,tsc->ntc", pieces, kernel)
    carried = product("mjkc,jkc->mkc", carry_table, span_states)
    across = product("mkc,tkc->mtc", carried * pole_weight[None], enter_table)
    piece = lax.all_gather(own_state[None], "ctx", axis=0, tiled=True)
    anchor = jnp.arange(piece.shape[0])
    distance = position - anchor - 1
    scaled = jnp.exp(
        -rate_table[None]
        * (row_count * jnp.maximum(distance, 0)).astype(jnp.float32)[:, None, None]
    )
    weight_rows = jnp.where((distance >= 0)[:, None, None], scaled, 0.0)
    gathered = jnp.sum(weight_rows * piece, axis=0)
    remote = product("mkc,tkc->mtc", powers * (pole_weight * gathered)[None], enter_table)
    response = skip_gain[None, :] * mixed_float + (within + across + remote).reshape(
        row_count, channels
    )
    layer_out = (outer_gate.astype(jnp.float32) * response).astype(jnp.bfloat16)
    grad_outer = (cotangent.astype(jnp.float32) * response).astype(jnp.bfloat16)
    grad_response = outer_gate.astype(jnp.float32) * cotangent.astype(jnp.float32)
    grad_pieces = grad_response.reshape(block_count, block_width, channels)
    span_adjoint = product("ntc,tkc->nkc", grad_pieces, enter_table)
    own_adjoint = jnp.sum(span_adjoint * powers, axis=0)
    within_back = product("ntc,tsc->nsc", grad_pieces, kernel)
    carried_back = product("mjkc,mkc->jkc", carry_table, span_adjoint)
    across_back = product("jkc,skc->jsc", carried_back * pole_weight[None], leave_table)
    piece = lax.all_gather(own_adjoint[None], "ctx", axis=0, tiled=True)
    anchor = jnp.arange(piece.shape[0])
    distance = anchor - position - 1
    scaled = jnp.exp(
        -rate_table[None]
        * (row_count * jnp.maximum(distance, 0)).astype(jnp.float32)[:, None, None]
    )
    weight_rows = jnp.where((distance >= 0)[:, None, None], scaled, 0.0)
    suffix = jnp.sum(weight_rows * piece, axis=0)
    decoded = product("nkc,skc->nsc", reverse_powers * (pole_weight * suffix)[None], leave_table)
    grad_mixed = skip_gain[None, :] * grad_response + (within_back + across_back + decoded).reshape(
        row_count, channels
    )
    grad_inner = (grad_mixed * values.astype(jnp.float32)).astype(jnp.bfloat16)
    grad_values = (grad_mixed * inner_gate.astype(jnp.float32)).astype(jnp.bfloat16)
    return (layer_out, grad_outer, grad_inner, grad_values)


def solution(mesh):
    return jax.shard_map(
        shards,
        mesh=mesh,
        in_specs=(
            P(("groups", "ctx"), None),
            P(("groups", "ctx"), None),
            P(("groups", "ctx"), None),
            P(("groups", "ctx"), None),
            P(),
            P(),
            P(),
        ),
        out_specs=(
            P(("groups", "ctx"), None),
            P(("groups", "ctx"), None),
            P(("groups", "ctx"), None),
            P(("groups", "ctx"), None),
        ),
        check_vma=False,
    )
```

profile of v0, /device:TPU:0, one launch (start us, length us, event | category | flops | bytes accessed | tf_op | source)
XLA Modules:
  0.0 141.4 jit_solution(13211322422101003060)
XLA Ops:
  0.6 0.0 copy-start.6
  0.6 0.0 copy-start.7
  0.7 0.5 iota_subtract_fusion.1
  1.2 0.6 multiply_convert_fusion
  1.8 0.6 fusion.40
  2.4 0.6 iota_compare_fusion.2
  3.0 0.6 convert_multiply_fusion.6
  3.6 0.7 negate_bitcast_fusion
  4.4 0.6 copy-done.8
  4.9 0.1 copy.58
  5.0 0.8 copy.57
  5.9 2.3 %multiply_reduce_fusion.4 = f32[64,256]{0,1:T(8,128)} fusion(f32[16,256]{0,1:T(8,128)S(1)} %copy.58, f32[16,256]{0,1:T(8,128)S(1)} %bitcast.60), kind=kLoop, calls=%fused_computation.26 | loop fusion | flops 770048 | bytes 98304 | tf_op jit(solution)/shard_map/reduce_sum | solution.py:31
  8.1 1.3 fusion.17
  9.5 0.0 copy-start.3
  9.5 1.0 copy.61
  10.5 1.1 convert_multiply_fusion
  11.6 2.5 %copy.68 = f32[16,64,256]{1,0,2:T(8,128)S(1)} copy(f32[16,64,256]{2,1,0:T(8,128)} %bitcast.59) | data formatting | bytes 2097152 | tf_op jit(solution)/shard_map/reshape | solution.py:59
  14.1 4.9 %fusion.14 = f32[64,64,256]{2,1,0:T(8,128)} fusion(s32[64,64]{1,0:T(8,128)S(1)} %iota_subtract_fusion, f32[64,256]{0,1:T(8,128)} %multiply_reduce_fusion.4), kind=kOutput, calls=%fused_computation.28 | convolution fusion | flops 805568512 | bytes 4276224 | tf_op jit(solution)/shard_map/tsl,lc->tsc/dot_general | solution.py:36
  19.0 9.1 %copy.60 = f32[64,64,256]{1,0,2:T(8,128)} copy(f32[64,64,256]{2,1,0:T(8,128)} %fusion.14) | data formatting | bytes 8388608 | tf_op jit(solution)/shard_map/tsl,lc->tsc/dot_general | solution.py:36
  28.2 4.0 %multiply_exponential_fusion = (f32[16,16,256]{1,0,2:T(8,128)}, f32[16,256]{0,1:T(8,128)S(1)}, f32[256,16,16]{1,2,0:T(8,128)}) fusion(f32[16]{0:T(128)S(1)} %iota_multiply_fusion, f32[16,256]{0,1:T(8,128)S(1)} %copy.58, f32[16,64,256]{1,0,2:T(8,128)S(1)} %copy.68, f32[64]{0:T(128)S(1)} %iota_add_fusion), kind=kOutput, calls=%fused_computation.20 | convolution fusion | flops 25620480 | bytes 1605952 | tf_op jit(solution)/shard_map/ntc,tkc->nkc/dot_general | solution.py:8
  32.2 2.4 %rev.3 = f32[16,16,256]{1,0,2:T(8,128)S(1)} reverse(f32[16,16,256]{1,0,2:T(8,128)} %get-tuple-element.12), dimensions={0} | reverse | bytes 524288 | tf_op jit(solution)/shard_map/rev | solution.py:25
  34.6 0.1 copy.70
  34.7 25.5 %all-gather.1 = f32[256,256]{1,0:T(8,128)} all-gather(f32[16,256]{1,0:T(8,128)S(1)} %copy.70), channel_id=3, replica_groups=mesh['groups'=2,'ctx'=16] {'ctx'}, dimensions={0}, use_global_device_ids=true | all-gather | bytes 278528 | tf_op jit(solution)/shard_map/all_gather | solution.py:65
  60.2 3.2 %copy.92 = f32[16,256,16]{1,0,2:T(8,128)} copy(f32[16,256,16]{0,2,1:T(8,128)} %bitcast.56) | data formatting | bytes 524288
  63.4 2.7 %multiply_reduce_fusion = f32[16,256,16]{1,0,2:T(8,128)} fusion(f32[16,256,16]{1,0,2:T(8,128)} %copy.92, f32[16,16]{1,0:T(8,128)S(1)} %copy-done.11, f32[16,256]{1,0:T(8,128)S(1)} %copy-done.9, pred[16,16]{1,0:T(8,128)(4,1)S(1)} %copy-done.17), kind=kLoop, calls=%fused_computation | loop fusion | flops 4128768 | bytes 541952
  66.1 3.4 %copy.89 = f32[16,256,16]{0,2,1:T(8,128)} copy(f32[16,256,16]{1,0,2:T(8,128)} %multiply_reduce_fusion) | data formatting | bytes 524288 | tf_op jit(solution)/shard_map/mjkc,mkc->jkc/dot_general | solution.py:8
  69.5 4.3 %fusion = f32[256,64,16]{1,2,0:T(8,128)} fusion(f32[16,256,16]{0,2,1:T(8,128)} %copy.89, f32[16,256]{0,1:T(8,128)S(1)} %bitcast.61, f32[64]{0:T(128)S(1)} %copy-done.13, f32[16,256]{0,1:T(8,128)S(1)} %copy.58), kind=kOutput, calls=%fused_computation.3 | convolution fusion | flops 25493504 | bytes 1343744 | tf_op jit(solution)/shard_map/jkc,skc->jsc/dot_general | solution.py:8
  73.7 3.4 %copy.71 = f32[16,16,256]{1,0,2:T(8,128)} copy(f32[16,16,256]{2,1,0:T(8,128)} %bitcast.63) | data formatting | bytes 524288 | tf_op jit(solution)/shard_map/all_gather | solution.py:65
  77.1 3.1 %fusion.5 = (f32[16,256]{0,1:T(8,128)S(1)}, f32[256,16,16]{1,2,0:T(8,128)}) fusion(f32[16,16,256]{1,0,2:T(8,128)S(1)} %rev.3, bf16[16,64,256]{1,0,2:T(8,128)(2,1)S(1)} %copy.61, f32[64]{0:T(128)S(1)} %copy-done.13, f32[16,256]{0,1:T(8,128)S(1)} %copy.58), kind=kOutput, calls=%fused_computation.10 | convolution fusion | flops 25554944 | bytes 1081600 | tf_op jit(solution)/shard_map/nsc,skc->nkc/dot_general | solution.py:8
  80.2 0.1 copy.64
  80.3 3.2 %copy.91 = f32[16,256,16]{1,0,2:T(8,128)} copy(f32[16,256,16]{0,2,1:T(8,128)} %bitcast.57) | data formatting | bytes 524288
  83.6 2.7 %multiply_reduce_fusion.1 = f32[16,256,16]{1,0,2:T(8,128)} fusion(f32[16,256,16]{1,0,2:T(8,128)} %copy.91, f32[16,16]{1,0:T(8,128)S(1)} %copy-done.12, f32[16,256]{1,0:T(8,128)S(1)} %copy-done.10, pred[16,16]{1,0:T(8,128)(4,1)S(1)} %copy-done.18), kind=kLoop, calls=%fused_computation.1 | loop fusion | flops 4128768 | bytes 541952
  86.3 19.5 %all-gather = f32[256,256]{1,0:T(8,128)} all-gather(f32[16,256]{1,0:T(8,128)S(1)} %copy.64), channel_id=2, replica_groups=mesh['groups'=2,'ctx'=16] {'ctx'}, dimensions={0}, use_global_device_ids=true | all-gather | bytes 278528 | tf_op jit(solution)/shard_map/all_gather | solution.py:43
  105.8 3.4 %copy.65 = f32[16,16,256]{1,0,2:T(8,128)} copy(f32[16,16,256]{2,1,0:T(8,128)} %bitcast.64) | data formatting | bytes 524288 | tf_op jit(solution)/shard_map/all_gather | solution.py:43
  109.2 3.9 %multiply_reduce_fusion.2 = (f32[16,256]{0,1:T(8,128)S(1)}, f32[16,256]{0,1:T(8,128)S(1)}) fusion(f32[16,16,256]{1,0,2:T(8,128)} %copy.71, f32[16]{0:T(128)S(1)} %copy-done.22, f32[16,256]{0,1:T(8,128)S(1)} %copy.58, pred[16]{0:T(512)(128)(4,1)S(1)} %copy-done.25, f32[16,16,256]{1,0,2:T(8,128)} %copy.65, f32[16]{0:T(128)S(1)} %copy-done.23, ...), kind=kLoop, calls=%fused_computation.14 | loop fusion | flops 516096 | bytes 573600 | tf_op jit(solution)/shard_map/reduce_sum | solution.py:73
  113.2 1.4 fusion.6
  114.6 0.2 copy-done.1
  114.8 0.6 copy-done.2
  115.4 5.8 %add_bitcast_fusion = f32[16,64,256]{1,0,2:T(8,128)S(1)} fusion(f32[256,64,16]{1,2,0:T(8,128)S(1)} %fusion.6, f32[256,64,16]{1,2,0:T(8,128)S(1)} %copy-done.2, f32[64,64,256]{1,0,2:T(8,128)} %copy.60, f32[16,64,256]{1,0,2:T(8,128)S(1)} %copy-done.1), kind=kOutput, calls=%fused_computation.11 | convolution fusion | flops 101187584 | bytes 8388608 | tf_op jit(solution)/shard_map/ntc,tsc->nsc/dot_general | solution.py:8
  121.2 2.1 %copy.72 = f32[16,64,256]{2,1,0:T(8,128)} copy(f32[16,64,256]{1,0,2:T(8,128)S(1)} %add_bitcast_fusion) | data formatting | bytes 2097152 | tf_op jit(solution)/shard_map/add | solution.py:75
  123.3 2.2 %copy.81 = f32[16,256,16]{0,2,1:T(8,128)S(1)} copy(f32[16,256,16]{1,0,2:T(8,128)} %multiply_reduce_fusion.1) | data formatting | bytes 524288 | tf_op jit(solution)/shard_map/mjkc,jkc->mkc/dot_general | solution.py:8
  125.5 1.4 fusion.3
  127.0 1.6 %fusion.9 = f32[256,64,16]{1,2,0:T(8,128)S(1)} fusion(f32[16,256]{0,1:T(8,128)S(1)} %get-tuple-element.15, f32[16]{0:T(128)S(1)} %copy-done.21, f32[16,256]{0,1:T(8,128)S(1)} %copy.58, f32[64]{0:T(128)S(1)} %copy-done.16), kind=kOutput, calls=%fused_computation.17 | convolution fusion | flops 25559040 | bytes 1081664 | tf_op jit(solution)/shard_map/mkc,tkc->mtc/dot_general | solution.py:8
  128.6 6.9 %add_bitcast_fusion.1 = f32[16,64,256]{1,0,2:T(8,128)S(1)} fusion(f32[256,64,16]{1,2,0:T(8,128)S(1)} %fusion.9, f32[256,64,16]{1,2,0:T(8,128)S(1)} %fusion.3, f32[64,64,256]{1,0,2:T(8,128)} %copy.60, bf16[16,64,256]{1,0,2:T(8,128)(2,1)S(1)} %copy.61), kind=kOutput, calls=%fused_computation.16 | convolution fusion | flops 101187584 | bytes 7864320 | tf_op jit(solution)/shard_map/nsc,tsc->ntc/dot_general | solution.py:8
  135.5 0.0 copy-start.4
  135.5 0.0 copy-start.5
  135.6 2.0 %copy.66 = f32[16,64,256]{2,1,0:T(8,128)} copy(f32[16,64,256]{1,0,2:T(8,128)S(1)} %add_bitcast_fusion.1) | data formatting | bytes 2097152 | tf_op jit(solution)/shard_map/add | solution.py:53
  137.6 3.8 %fusion.19 = (bf16[1024,256]{1,0:T(8,128)(2,1)}, bf16[1024,256]{1,0:T(8,128)(2,1)}, bf16[1024,256]{1,0:T(8,128)(2,1)}, bf16[1024,256]{1,0:T(8,128)(2,1)}) fusion(bf16[1024,256]{1,0:T(8,128)(2,1)} %param.10, f32[16,64,256]{2,1,0:T(8,128)} %copy.66, bf16[1024,256]{1,0:T(8,128)(2,1)S(1)} %copy-done.4, f32[256]{0:T(256)S(1)} %copy-done.19, ...), kind=kLoop, calls=%fused_computation.39 | loop fusion | flops 4718592 | bytes 6816768 | tf_op jit(solution)/shard_map/convert_element_type | solution.py:57
  (48 shorter events, 0.1 us)
Async XLA Ops:
  0.6 9.8 %copy-start.6 = (bf16[1024,256]{1,0:T(8,128)(2,1)S(1)}, bf16[1024,256]{1,0:T(8,128)(2,1)}, u32[]{:S(2)}) copy-start(bf16[1024,256]{1,0:T(8,128)(2,1)} %param.10) | copy-start | bytes 1572868
  0.6 9.8 %copy-start.7 = (bf16[1024,256]{1,0:T(8,128)(2,1)S(1)}, bf16[1024,256]{1,0:T(8,128)(2,1)}, u32[]{:S(2)}) copy-start(bf16[1024,256]{1,0:T(8,128)(2,1)} %param.7) | copy-start | bytes 1572868
  0.7 27.5 %copy-start.15 = (f32[64]{0:T(128)}, f32[64]{0:T(128)S(1)}, u32[]{:S(2)}) copy-start(f32[64]{0:T(128)S(1)} %iota_add_fusion) | copy-start | bytes 772
  1.2 26.9 %copy-start.20 = (f32[16]{0:T(128)}, f32[16]{0:T(128)S(1)}, u32[]{:S(2)}) copy-start(f32[16]{0:T(128)S(1)} %iota_multiply_fusion) | copy-start | bytes 196
  4.3 0.6 copy-start.8
  9.5 2.1 %copy-start.3 = (bf16[1024,256]{1,0:T(8,128)(2,1)}, bf16[1024,256]{1,0:T(8,128)(2,1)S(1)}, u32[]{:S(2)}) copy-start(bf16[1024,256]{1,0:T(8,128)(2,1)S(1)} %fusion.17) | copy-start | bytes 1572868
  14.1 14.1 %copy-start = (f32[16,64,256]{1,0,2:T(8,128)}, f32[16,64,256]{1,0,2:T(8,128)S(1)}, u32[]{:S(2)}) copy-start(f32[16,64,256]{1,0,2:T(8,128)S(1)} %copy.68) | copy-start | bytes 3145732
  34.6 28.7 %copy-start.9 = (f32[16,256]{1,0:T(8,128)S(1)}, f32[16,256]{1,0:T(8,128)}, u32[]{:S(2)}) copy-start(f32[16,256]{1,0:T(8,128)} %copy-done.8) | copy-start | bytes 49156
  34.6 28.7 %copy-start.11 = (f32[16,16]{1,0:T(8,128)S(1)}, f32[16,16]{1,0:T(8,128)}, u32[]{:S(2)}) copy-start(f32[16,16]{1,0:T(8,128)} %convert_multiply_fusion.6) | copy-start | bytes 3076
  34.6 28.7 %copy-start.17 = (pred[16,16]{1,0:T(8,128)(4,1)S(1)}, pred[16,16]{1,0:T(8,128)(4,1)}, u32[]{:S(2)}) copy-start(pred[16,16]{1,0:T(8,128)(4,1)} %iota_compare_fusion.2) | copy-start | bytes 772
  63.4 6.1 %copy-start.13 = (f32[64]{0:T(128)S(1)}, f32[64]{0:T(128)}, u32[]{:S(2)}) copy-start(f32[64]{0:T(128)} %iota_subtract_fusion.1) | copy-start | bytes 772
  80.3 3.2 %copy-start.10 = (f32[16,256]{1,0:T(8,128)S(1)}, f32[16,256]{1,0:T(8,128)}, u32[]{:S(2)}) copy-start(f32[16,256]{1,0:T(8,128)} %copy-done.8) | copy-start | bytes 49156
  80.3 3.2 %copy-start.12 = (f32[16,16]{1,0:T(8,128)S(1)}, f32[16,16]{1,0:T(8,128)}, u32[]{:S(2)}) copy-start(f32[16,16]{1,0:T(8,128)} %convert_multiply_fusion.6) | copy-start | bytes 3076
  80.3 3.2 %copy-start.18 = (pred[16,16]{1,0:T(8,128)(4,1)S(1)}, pred[16,16]{1,0:T(8,128)(4,1)}, u32[]{:S(2)}) copy-start(pred[16,16]{1,0:T(8,128)(4,1)} %iota_compare_fusion.2) | copy-start | bytes 772
  83.5 25.7 %copy-start.22 = (f32[16]{0:T(128)S(1)}, f32[16]{0:T(128)}, u32[]{:S(2)}) copy-start(f32[16]{0:T(128)} %get-tuple-element.19) | copy-start | bytes 196
  83.5 25.7 %copy-start.23 = (f32[16]{0:T(128)S(1)}, f32[16]{0:T(128)}, u32[]{:S(2)}) copy-start(f32[16]{0:T(128)} %get-tuple-element.20) | copy-start | bytes 196
  83.5 25.7 %copy-start.24 = (pred[16]{0:T(512)(128)(4,1)S(1)}, pred[16]{0:T(512)(128)(4,1)}, u32[]{:S(2)}) copy-start(pred[16]{0:T(512)(128)(4,1)} %get-tuple-element.21) | copy-start | bytes 52
  83.6 25.7 %copy-start.25 = (pred[16]{0:T(512)(128)(4,1)S(1)}, pred[16]{0:T(512)(128)(4,1)}, u32[]{:S(2)}) copy-start(pred[16]{0:T(512)(128)(4,1)} %get-tuple-element.22) | copy-start | bytes 52
  109.2 3.9 %copy-start.14 = (f32[64]{0:T(128)S(1)}, f32[64]{0:T(128)}, u32[]{:S(2)}) copy-start(f32[64]{0:T(128)} %iota_subtract_fusion.1) | copy-start | bytes 772
  113.2 1.6 %copy-start.1 = (f32[16,64,256]{1,0,2:T(8,128)S(1)}, f32[16,64,256]{1,0,2:T(8,128)}, u32[]{:S(2)}) copy-start(f32[16,64,256]{1,0,2:T(8,128)} %copy-done) | copy-start | bytes 3145732
  113.2 2.2 %copy-start.2 = (f32[256,64,16]{1,2,0:T(8,128)S(1)}, f32[256,64,16]{1,2,0:T(8,128)}, u32[]{:S(2)}) copy-start(f32[256,64,16]{1,2,0:T(8,128)} %fusion) | copy-start | bytes 3145732
  121.2 4.3 %copy-start.16 = (f32[64]{0:T(128)S(1)}, f32[64]{0:T(128)}, u32[]{:S(2)}) copy-start(f32[64]{0:T(128)} %copy-done.15) | copy-start | bytes 772
  125.5 1.4 copy-start.21
  135.5 2.0 %copy-start.4 = (bf16[1024,256]{1,0:T(8,128)(2,1)S(1)}, bf16[1024,256]{1,0:T(8,128)(2,1)}, u32[]{:S(2)}) copy-start(bf16[1024,256]{1,0:T(8,128)(2,1)} %copy-done.3) | copy-start | bytes 1572868
  135.5 2.0 %copy-start.5 = (bf16[1024,256]{1,0:T(8,128)(2,1)S(1)}, bf16[1024,256]{1,0:T(8,128)(2,1)}, u32[]{:S(2)}) copy-start(bf16[1024,256]{1,0:T(8,128)(2,1)} %param.9) | copy-start | bytes 1572868
  135.5 2.0 %copy-start.19 = (f32[256]{0:T(256)S(1)}, f32[256]{0:T(256)}, u32[]{:S(2)}) copy-start(f32[256]{0:T(256)} %param.13) | copy-start | bytes 3076
where the time goes:
time: 142 us; the launch traced here: 141 us
  blocking collectives  45.1 us (32%)
  local copies, waits for them, and re-layouts  40.4 us (28%)
  matrix products  33.5 us (24%)
  other arithmetic  21.5 us (15%)
    dot_general x8, matrix products, product(): return jnp.einsum(pattern, first, second, precision=lax.Precision.HIGH)  28.6 us
    all_gather x1, blocking collectives, shards(): piece = lax.all_gather(own_adjoint[None], 'ctx', axis=0, tiled=True)  25.5 us
    all_gather x1, blocking collectives, shards(): piece = lax.all_gather(own_state[None], 'ctx', axis=0, tiled=True)  19.5 us
    dot_general x1, local copies, waits for them, and re-layouts, shards(): jnp.einsum('tsl,lc->tsc', lag_onehot, tap_values, precision=lax.Precision...  9.14 us
    unnamed x55, local copies, waits for them, and re-layouts  8.71 us
    dot_general x2, local copies, waits for them, and re-layouts, product(): return jnp.einsum(pattern, first, second, precision=lax.Precision.HIGH)  5.63 us
    unnamed x2, other arithmetic  5.42 us
    dot_general x1, matrix products, shards(): jnp.einsum('tsl,lc->tsc', lag_onehot, tap_values, precision=lax.Precision...  4.9 us

commit v1 on v0

--- a/solution.py
+++ b/solution.py
@@ -1,7 +1,46 @@
+import functools
 import jax
 import jax.numpy as jnp
 from jax import lax
 from jax.sharding import PartitionSpec as P
+from jax.lax import axis_index, ppermute, psum
+
+
+def process_sources_all(q_in, along_dim):
+    found_now = list(q_in.shape[1:])
+    found_now[along_dim] *= q_in.shape[0]
+    return jnp.moveaxis(q_in, 0, along_dim).reshape(found_now)
+
+
+def axis_part_prepare(shard_in, a_name, at_axis):
+    table = []
+    t = 0
+    extent = psum(1, a_name)
+    while t < extent:
+        table.append((t, (t + 1) % extent))
+        t = t + 1
+    in_order = []
+    for w, b in table:
+        in_order.append((b, w))
+    mat_out, current_block = ([], [])
+    src_i = 0
+    while src_i < extent - 1:
+        if src_i % 2 == 0:
+            b_next = ppermute(mat_out[-1] if mat_out else shard_in, a_name, table)
+            mat_out.append(b_next)
+        else:
+            vec_out = ppermute(current_block[-1] if current_block else shard_in, a_name, in_order)
+            current_block.append(vec_out)
+        src_i += 1
+    view_out = jnp.stack([*mat_out[::-1], shard_in, *current_block])
+    before = axis_index(a_name)
+    then = len(mat_out)
+    n_now = before - then
+    view_out = view_out[(jnp.arange(extent) - n_now) % extent]
+    return process_sources_all(view_out, at_axis)
+
+
+treat_the_zone = functools.partial(axis_part_prepare, a_name="ctx", at_axis=0)
 
 
 def product(pattern, first, second):
@@ -40,7 +79,7 @@
     within = product("nsc,tsc->ntc", pieces, kernel)
     carried = product("mjkc,jkc->mkc", carry_table, span_states)
     across = product("mkc,tkc->mtc", carried * pole_weight[None], enter_table)
-    piece = lax.all_gather(own_state[None], "ctx", axis=0, tiled=True)
+    piece = treat_the_zone(own_state[None])
     anchor = jnp.arange(piece.shape[0])
     distance = position - anchor - 1
     scaled = jnp.exp(

time: 142 us -> 175 us (1.23)
  starting transfers between devices: 0 us -> 28.8 us
  blocking collectives: 45.1 us -> 20.1 us
  local copies, waits for them, and re-layouts: 40.4 us -> 57.8 us
  waiting for transfers between devices: 0 us -> 9.3 us
  matrix products: 33.5 us -> 36.2 us
    ppermute x0 -> x15, starting transfers between devices: none -> 28.8 us  [the longest x7 28.8 us: axis_part_prepare(): ppermute(current_block[-1] if current_block else shard_in, a_name, in_order)]
    all_gather x1 -> x0, blocking collectives: 19.5 us -> none  [shards(): piece = lax.all_gather(own_state[None], 'ctx', axis=0, tiled=True)]
    unnamed x55 -> x62, local copies, waits for them, and re-layouts: 8.71 us -> 20.7 us
    ppermute x0 -> x15, waiting for transfers between devices: none -> 9.3 us  [the longest x8 6.17 us: axis_part_prepare(): b_next = ppermute(mat_out[-1] if mat_out else shard_in, a_name, table)]
    gather x0 -> x2, local copies, waits for them, and re-layouts: none -> 5.75 us  [axis_part_prepare(): view_out = view_out[(jnp.arange(extent) - n_now) % extent]]
    all_gather x1, blocking collectives: 25.5 us -> 20.1 us  [shards(): piece = lax.all_gather(own_adjoint[None], 'ctx', axis=0, tiled=True)]
    dot_general x8, matrix products: 28.6 us -> 32.4 us  [product(): return jnp.einsum(pattern, first, second, precision=lax.Precision.HIGH)]
    all_gather x1 -> x0, local copies, waits for them, and re-layouts: 3.37 us -> none  [shards(): piece = lax.all_gather(own_state[None], 'ctx', axis=0, tiled=True)]
  transfers between devices with their start and end apart: 0 -> 15, of which waited for: 0 -> 4; matrix products, arithmetic and copies ran while one was open for 0% -> 35% of each run, Pallas kernels for 0% -> 0%
where the time goes in v1:
time: 175 us; the launch traced here: 174 us
  local copies, waits for them, and re-layouts  57.8 us (33%)
  matrix products  36.2 us (21%)
  starting transfers between devices  28.8 us (16%)
  other arithmetic  21.2 us (12%)
  blocking collectives  20.1 us (11%)
  waiting for transfers between devices  9.3 us (5%)
    dot_general x8, matrix products, product(): return jnp.einsum(pattern, first, second, precision=lax.Precision.HIGH)  32.4 us
    ppermute x7, starting transfers between devices, axis_part_prepare(): ppermute(current_block[-1] if current_block else shard_in, a_name, in_order)  28.8 us
    unnamed x62, local copies, waits for them, and re-layouts  20.7 us
    all_gather x1, blocking collectives, shards(): piece = lax.all_gather(own_adjoint[None], 'ctx', axis=0, tiled=True)  20.1 us
    dot_general x1, local copies, waits for them, and re-layouts, shards(): jnp.einsum('tsl,lc->tsc', lag_onehot, tap_values, precision=lax.Precision...  9.16 us
    dot_general x2, local copies, waits for them, and re-layouts, product(): return jnp.einsum(pattern, first, second, precision=lax.Precision.HIGH)  6.8 us
    ppermute x8, waiting for transfers between devices, axis_part_prepare(): b_next = ppermute(mat_out[-1] if mat_out else shard_in, a_name, table)  6.17 us
    gather x2, local copies, waits for them, and re-layouts, axis_part_prepare(): view_out = view_out[(jnp.arange(extent) - n_now) % extent]  5.75 us
  transfers between devices with their start and end apart: 15, of which 4 were waited for; matrix products, arithmetic and copies ran while one was open for 35% of the time, Pallas kernels for 0%

profile of v1, /device:TPU:0, one launch (start us, length us, event | category | flops | bytes accessed | tf_op | source)
XLA Modules:
  0.0 174.3 jit_solution(6533165474000009464)
XLA Ops:
  2.0 1.3 fusion.17
  3.4 1.0 copy.91
  4.4 1.1 convert_multiply_fusion
  5.5 2.5 %copy.113 = f32[16,64,256]{1,0,2:T(8,128)S(1)} copy(f32[16,64,256]{2,1,0:T(8,128)} %bitcast.122) | data formatting | bytes 2097152 | tf_op jit(solution)/shard_map/reshape | solution.py:98
  8.0 4.1 %multiply_exponential_fusion = (f32[16,16,256]{1,0,2:T(8,128)}, f32[16,256]{0,1:T(8,128)S(1)}, f32[256,16,16]{1,2,0:T(8,128)}) fusion(f32[16]{0:T(128)S(1)} %iota_multiply_fusion, f32[16,256]{0,1:T(8,128)S(1)} %copy.88, f32[16,64,256]{1,0,2:T(8,128)S(1)} %copy.113, f32[64]{0:T(128)S(1)} %iota_add_fusion), kind=kOutput, calls=%fused_computation.21 | convolution fusion | flops 25620480 | bytes 1605952 | tf_op jit(solution)/shard_map/ntc,tkc->nkc/dot_general | solution.py:47
  12.1 2.4 %rev.3 = f32[16,16,256]{1,0,2:T(8,128)S(1)} reverse(f32[16,16,256]{1,0,2:T(8,128)} %get-tuple-element.12), dimensions={0} | reverse | bytes 524288 | tf_op jit(solution)/shard_map/rev | solution.py:64
  14.5 3.7 %fusion.5 = (f32[16,256]{0,1:T(8,128)S(1)}, f32[256,16,16]{1,2,0:T(8,128)}) fusion(f32[16,16,256]{1,0,2:T(8,128)S(1)} %rev.3, bf16[16,64,256]{1,0,2:T(8,128)(2,1)S(1)} %copy.91, f32[64]{0:T(128)} %iota_subtract_fusion.1, f32[16,256]{0,1:T(8,128)S(1)} %copy.88), kind=kOutput, calls=%fused_computation.11 | convolution fusion | flops 25554944 | bytes 1081600 | tf_op jit(solution)/shard_map/nsc,skc->nkc/dot_general | solution.py:47
  18.8 5.4 %collective-permute-start.8 = (f32[1,16,256]{2,1,0:T(8,128)}, f32[1,16,256]{2,1,0:T(8,128)}, u32[]{:S(2)}, u32[]{:S(2)}) collective-permute-start(f32[1,16,256]{2,1,0:T(8,128)} %bitcast.11), channel_id=1, source_target_pairs={{1,0},{2,1},{3,2},{4,3},{5,4},{6,5},{7,6},{8,7},{9,8},{10,9},{11,1... | collective-permute-start | bytes 49160 | tf_op jit(solution)/shard_map/ppermute | solution.py:32
  25.5 0.8 copy.87
  26.3 3.2 %copy.137 = f32[16,256,16]{1,0,2:T(8,128)} copy(f32[16,256,16]{0,2,1:T(8,128)} %bitcast.119) | data formatting | bytes 524288
  29.5 2.7 %multiply_reduce_fusion = f32[16,256,16]{1,0,2:T(8,128)} fusion(f32[16,256,16]{1,0,2:T(8,128)} %copy.137, f32[16,16]{1,0:T(8,128)} %convert_multiply_fusion.6, f32[16,256]{1,0:T(8,128)S(1)} %negate_bitcast_fusion, pred[16,16]{1,0:T(8,128)(4,1)} %iota_compare_fusion.2), kind=kLoop, calls=%fused_computation.1 | loop fusion | flops 4128768 | bytes 541952
  32.1 3.4 %copy.134 = f32[16,256,16]{0,2,1:T(8,128)} copy(f32[16,256,16]{1,0,2:T(8,128)} %multiply_reduce_fusion) | data formatting | bytes 524288 | tf_op jit(solution)/shard_map/mjkc,mkc->jkc/dot_general | solution.py:47
  35.5 3.2 %copy.136 = f32[16,256,16]{1,0,2:T(8,128)} copy(f32[16,256,16]{0,2,1:T(8,128)} %bitcast.120) | data formatting | bytes 524288
  38.7 2.8 %multiply_reduce_fusion.1 = f32[16,256,16]{1,0,2:T(8,128)} fusion(f32[16,256,16]{1,0,2:T(8,128)} %copy.136, f32[16,16]{1,0:T(8,128)} %convert_multiply_fusion.6, f32[16,256]{1,0:T(8,128)S(1)} %negate_bitcast_fusion, pred[16,16]{1,0:T(8,128)(4,1)} %iota_compare_fusion.2), kind=kLoop, calls=%fused_computation.2 | loop fusion | flops 4128768 | bytes 541952
  41.5 3.4 %copy.126 = f32[16,256,16]{0,2,1:T(8,128)} copy(f32[16,256,16]{1,0,2:T(8,128)} %multiply_reduce_fusion.1) | data formatting | bytes 524288 | tf_op jit(solution)/shard_map/mjkc,jkc->mkc/dot_general | solution.py:47
  44.9 4.4 %fusion = f32[256,64,16]{1,2,0:T(8,128)} fusion(f32[16,256,16]{0,2,1:T(8,128)} %copy.134, f32[16,256]{0,1:T(8,128)S(1)} %bitcast.123, f32[64]{0:T(128)S(1)} %copy-done.10, f32[16,256]{0,1:T(8,128)S(1)} %copy.88), kind=kOutput, calls=%fused_computation.4 | convolution fusion | flops 25493504 | bytes 1343744 | tf_op jit(solution)/shard_map/jkc,skc->jsc/dot_general | solution.py:47
  49.3 2.5 %fusion.3 = f32[256,64,16]{1,2,0:T(8,128)} fusion(f32[16,256,16]{0,2,1:T(8,128)S(1)} %copy-done.3, f32[16,256]{0,1:T(8,128)S(1)} %bitcast.124, f32[64]{0:T(128)S(1)} %copy-done.13, f32[16,256]{0,1:T(8,128)S(1)} %copy.88), kind=kOutput, calls=%fused_computation.8 | convolution fusion | flops 25493504 | bytes 1343744 | tf_op jit(solution)/shard_map/mkc,tkc->mtc/dot_general | solution.py:47
  51.8 1.6 multiply_reduce_fusion.4
  53.5 6.2 %collective-permute-done.1 = f32[1,16,256]{2,1,0:T(8,128)} collective-permute-done((f32[1,16,256]{2,1,0:T(8,128)}, f32[1,16,256]{2,1,0:T(8,128)}, u32[]{:S(2)}, u32[]{:S(2)}) %collective-permute-start.1) | collective-permute-done | bytes 16416 | tf_op jit(solution)/shard_map/ppermute | solution.py:29
  59.7 3.8 %fusion.14 = f32[64,64,256]{2,1,0:T(8,128)} fusion(s32[64,64]{1,0:T(8,128)S(1)} %iota_subtract_fusion, f32[64,256]{0,1:T(8,128)S(1)} %multiply_reduce_fusion.4), kind=kOutput, calls=%fused_computation.29 | convolution fusion | flops 805568512 | bytes 4276224 | tf_op jit(solution)/shard_map/tsl,lc->tsc/dot_general | solution.py:75
  63.5 4.5 %collective-permute-start.9 = (f32[1,16,256]{2,1,0:T(8,128)}, f32[1,16,256]{2,1,0:T(8,128)S(1)}, u32[]{:S(2)}, u32[]{:S(2)}) collective-permute-start(f32[1,16,256]{2,1,0:T(8,128)} %collective-permute-done.8), channel_id=1, source_target_pairs={{1,0},{2,1},{3,2},{4,3},{5,4},{6,5},{7,6},{8,7},{9,8},{10,9},{11,1... | collective-permute-start | bytes 49160 | tf_op jit(solution)/shard_map/ppermute | solution.py:32
  68.0 20.1 %all-gather = f32[256,256]{1,0:T(8,128)} all-gather(f32[16,256]{1,0:T(8,128)S(1)} %copy.115), channel_id=2, replica_groups=mesh['groups'=2,'ctx'=16] {'ctx'}, dimensions={0}, use_global_device_ids=true | all-gather | bytes 278528 | tf_op jit(solution)/shard_map/all_gather | solution.py:104
  88.1 1.2 collective-permute-start.10
  89.3 1.4 collective-permute-done.10
  90.7 4.4 %collective-permute-start.11 = (f32[1,16,256]{2,1,0:T(8,128)S(1)}, f32[1,16,256]{2,1,0:T(8,128)S(1)}, u32[]{:S(2)}, u32[]{:S(2)}) collective-permute-start(f32[1,16,256]{2,1,0:T(8,128)S(1)} %collective-permute-done.10), channel_id=1, source_target_pairs={{1,0},{2,1},{3,2},{4,3},{5,4},{6,5},{7,6},{8,7},{9,8},{10,9},{11,1... | collective-permute-start | bytes 49160 | tf_op jit(solution)/shard_map/ppermute | solution.py:32
  95.8 0.8 collective-permute-done.11
  96.6 4.4 %collective-permute-start.12 = (f32[1,16,256]{2,1,0:T(8,128)S(1)}, f32[1,16,256]{2,1,0:T(8,128)S(1)}, u32[]{:S(2)}, u32[]{:S(2)}) collective-permute-start(f32[1,16,256]{2,1,0:T(8,128)S(1)} %collective-permute-done.11), channel_id=1, source_target_pairs={{1,0},{2,1},{3,2},{4,3},{5,4},{6,5},{7,6},{8,7},{9,8},{10,9},{11,1... | collective-permute-start | bytes 49160 | tf_op jit(solution)/shard_map/ppermute | solution.py:32
  101.6 0.9 collective-permute-done.12
  102.5 4.4 %collective-permute-start.13 = (f32[1,16,256]{2,1,0:T(8,128)S(1)}, f32[1,16,256]{2,1,0:T(8,128)S(1)}, u32[]{:S(2)}, u32[]{:S(2)}) collective-permute-start(f32[1,16,256]{2,1,0:T(8,128)S(1)} %collective-permute-done.12), channel_id=1, source_target_pairs={{1,0},{2,1},{3,2},{4,3},{5,4},{6,5},{7,6},{8,7},{9,8},{10,9},{11,1... | collective-permute-start | bytes 49160 | tf_op jit(solution)/shard_map/ppermute | solution.py:32
  107.5 9.2 %copy.90 = f32[64,64,256]{1,0,2:T(8,128)} copy(f32[64,64,256]{2,1,0:T(8,128)} %fusion.14) | data formatting | bytes 8388608 | tf_op jit(solution)/shard_map/tsl,lc->tsc/dot_general | solution.py:75
  116.6 3.5 %copy.116 = f32[16,16,256]{1,0,2:T(8,128)} copy(f32[16,16,256]{2,1,0:T(8,128)} %bitcast.126) | data formatting | bytes 524288 | tf_op jit(solution)/shard_map/all_gather | solution.py:104
  120.1 4.4 %collective-permute-start.14 = (f32[1,16,256]{2,1,0:T(8,128)S(1)}, f32[1,16,256]{2,1,0:T(8,128)S(1)}, u32[]{:S(2)}, u32[]{:S(2)}) collective-permute-start(f32[1,16,256]{2,1,0:T(8,128)S(1)} %collective-permute-done.13), channel_id=1, source_target_pairs={{1,0},{2,1},{3,2},{4,3},{5,4},{6,5},{7,6},{8,7},{9,8},{10,9},{11,1... | collective-permute-start | bytes 49160 | tf_op jit(solution)/shard_map/ppermute | solution.py:32
  124.5 1.3 constant_dynamic-update-slice_fusion.15
  128.3 1.3 constant_dynamic-update-slice_fusion.10
  129.6 1.3 constant_dynamic-update-slice_fusion.9
  130.9 1.3 constant_dynamic-update-slice_fusion.8
  132.3 1.3 constant_dynamic-update-slice_fusion.7
  133.6 1.3 constant_dynamic-update-slice_fusion.6
  138.6 2.3 %gather_fusion = f32[16,16,256]{2,1,0:T(8,128)} fusion(f32[16,16,256]{2,1,0:T(8,128)} %bitcast.42, s32[1024]{0:T(1024)} %pad_clamp_fusion), kind=kCustom, calls=%fused_computation | custom fusion | bytes 524352 | tf_op jit(solution)/shard_map/gather | solution.py:39
  140.9 3.4 %copy.110 = f32[16,16,256]{1,0,2:T(8,128)} copy(f32[16,16,256]{2,1,0:T(8,128)} %gather_fusion) | data formatting | bytes 524288 | tf_op jit(solution)/shard_map/gather | solution.py:39
  144.3 4.0 %multiply_reduce_fusion.2 = (f32[16,256]{0,1:T(8,128)S(1)}, f32[16,256]{0,1:T(8,128)S(1)}) fusion(f32[16,16,256]{1,0,2:T(8,128)} %copy.116, f32[16]{0:T(128)S(1)} %copy-done.18, f32[16,256]{0,1:T(8,128)S(1)} %copy.88, pred[16]{0:T(512)(128)(4,1)S(1)} %copy-done.21, f32[16,16,256]{1,0,2:T(8,128)} %copy.110, f32[16]{0:T(128)S(1)} %copy-done.19, ...), kind=kLoop, calls=%fused_computation.15 | loop fusion | flops 516096 | bytes 573600 | tf_op jit(solution)/shard_map/reduce_sum | solution.py:112
  148.4 1.4 fusion.6
  149.8 5.4 %add_bitcast_fusion = f32[16,64,256]{1,0,2:T(8,128)S(1)} fusion(f32[256,64,16]{1,2,0:T(8,128)S(1)} %fusion.6, f32[256,64,16]{1,2,0:T(8,128)} %fusion, f32[64,64,256]{1,0,2:T(8,128)S(1)} %copy-done, f32[16,64,256]{1,0,2:T(8,128)} %copy-done.1), kind=kOutput, calls=%fused_computation.12 | convolution fusion | flops 101187584 | bytes 8388608 | tf_op jit(solution)/shard_map/ntc,tsc->nsc/dot_general | solution.py:47
  155.3 2.0 %copy.117 = f32[16,64,256]{2,1,0:T(8,128)} copy(f32[16,64,256]{1,0,2:T(8,128)S(1)} %add_bitcast_fusion) | data formatting | bytes 2097152 | tf_op jit(solution)/shard_map/add | solution.py:114
  157.3 1.6 fusion.9
  158.9 9.3 %add_bitcast_fusion.1 = f32[16,64,256]{1,0,2:T(8,128)} fusion(f32[256,64,16]{1,2,0:T(8,128)S(1)} %fusion.9, f32[256,64,16]{1,2,0:T(8,128)S(1)} %copy-done.2, f32[64,64,256]{1,0,2:T(8,128)} %copy.90, bf16[16,64,256]{1,0,2:T(8,128)(2,1)S(1)} %copy.91), kind=kOutput, calls=%fused_computation.17 | convolution fusion | flops 101187584 | bytes 7864320 | tf_op jit(solution)/shard_map/nsc,tsc->ntc/dot_general | solution.py:47
  168.2 2.7 %copy.111 = f32[16,64,256]{2,1,0:T(8,128)S(1)} copy(f32[16,64,256]{1,0,2:T(8,128)} %add_bitcast_fusion.1) | data formatting | bytes 2097152 | tf_op jit(solution)/shard_map/add | solution.py:92
  170.9 3.4 %fusion.19 = (bf16[1024,256]{1,0:T(8,128)(2,1)}, bf16[1024,256]{1,0:T(8,128)(2,1)}, bf16[1024,256]{1,0:T(8,128)(2,1)}, bf16[1024,256]{1,0:T(8,128)(2,1)}) fusion(bf16[1024,256]{1,0:T(8,128)(2,1)} %param.10, f32[16,64,256]{2,1,0:T(8,128)S(1)} %copy.111, bf16[1024,256]{1,0:T(8,128)(2,1)S(1)} %copy-done.5, f32[256]{0:T(256)S(1)} %copy-done.15, ...), kind=kLoop, calls=%fused_computation.40 | loop fusion | flops 4718592 | bytes 6816768 | tf_op jit(solution)/shard_map/convert_element_type | solution.py:96
  (88 shorter events, 11.4 us)
Async XLA Ops:
  0.6 3.7 %copy-start.8 = (bf16[1024,256]{1,0:T(8,128)(2,1)S(1)}, bf16[1024,256]{1,0:T(8,128)(2,1)}, u32[]{:S(2)}) copy-start(bf16[1024,256]{1,0:T(8,128)(2,1)} %param.10) | copy-start | bytes 1572868
  0.6 3.7 %copy-start.9 = (bf16[1024,256]{1,0:T(8,128)(2,1)S(1)}, bf16[1024,256]{1,0:T(8,128)(2,1)}, u32[]{:S(2)}) copy-start(bf16[1024,256]{1,0:T(8,128)(2,1)} %param.7) | copy-start | bytes 1572868
  0.7 7.3 %copy-start.12 = (f32[64]{0:T(128)}, f32[64]{0:T(128)S(1)}, u32[]{:S(2)}) copy-start(f32[64]{0:T(128)S(1)} %iota_add_fusion) | copy-start | bytes 772
  1.2 6.8 %copy-start.16 = (f32[16]{0:T(128)}, f32[16]{0:T(128)S(1)}, u32[]{:S(2)}) copy-start(f32[16]{0:T(128)S(1)} %iota_multiply_fusion) | copy-start | bytes 196
  3.4 2.1 %copy-start.4 = (bf16[1024,256]{1,0:T(8,128)(2,1)}, bf16[1024,256]{1,0:T(8,128)(2,1)S(1)}, u32[]{:S(2)}) copy-start(bf16[1024,256]{1,0:T(8,128)(2,1)S(1)} %fusion.17) | copy-start | bytes 1572868
  8.0 4.1 %copy-start.1 = (f32[16,64,256]{1,0,2:T(8,128)}, f32[16,64,256]{1,0,2:T(8,128)S(1)}, u32[]{:S(2)}) copy-start(f32[16,64,256]{1,0,2:T(8,128)S(1)} %copy.113) | copy-start | bytes 3145732
  18.8 44.7 %collective-permute-start.8 = (f32[1,16,256]{2,1,0:T(8,128)}, f32[1,16,256]{2,1,0:T(8,128)}, u32[]{:S(2)}, u32[]{:S(2)}) collective-permute-start(f32[1,16,256]{2,1,0:T(8,128)} %bitcast.11), channel_id=1, source_target_pairs={{1,0},{2,1},{3,2},{4,3},{5,4},{6,5},{7,6},{8,7},{9,8},{10,9},{11,1... | collective-permute-start | bytes 49160 | tf_op jit(solution)/shard_map/ppermute | solution.py:32
  24.3 29.2 %collective-permute-start = (f32[1,16,256]{2,1,0:T(8,128)}, f32[1,16,256]{2,1,0:T(8,128)}, u32[]{:S(2)}, u32[]{:S(2)}) collective-permute-start(f32[1,16,256]{2,1,0:T(8,128)} %bitcast.11), channel_id=1, source_target_pairs={{0,1},{1,2},{2,3},{3,4},{4,5},{5,6},{6,7},{7,8},{8,9},{9,10},{10,1... | collective-permute-start | bytes 49160 | tf_op jit(solution)/shard_map/ppermute | solution.py:29
  41.5 3.4 %copy-start.10 = (f32[64]{0:T(128)S(1)}, f32[64]{0:T(128)}, u32[]{:S(2)}) copy-start(f32[64]{0:T(128)} %iota_subtract_fusion.1) | copy-start | bytes 772
  44.9 4.4 %copy-start.3 = (f32[16,256,16]{0,2,1:T(8,128)S(1)}, f32[16,256,16]{0,2,1:T(8,128)}, u32[]{:S(2)}) copy-start(f32[16,256,16]{0,2,1:T(8,128)} %copy.126) | copy-start | bytes 786436
  44.9 4.4 %copy-start.13 = (f32[64]{0:T(128)S(1)}, f32[64]{0:T(128)}, u32[]{:S(2)}) copy-start(f32[64]{0:T(128)} %copy-done.12) | copy-start | bytes 772
  53.4 6.2 %collective-permute-start.1 = (f32[1,16,256]{2,1,0:T(8,128)}, f32[1,16,256]{2,1,0:T(8,128)}, u32[]{:S(2)}, u32[]{:S(2)}) collective-permute-start(f32[1,16,256]{2,1,0:T(8,128)} %collective-permute-done), channel_id=1, source_target_pairs={{0,1},{1,2},{2,3},{3,4},{4,5},{5,6},{6,7},{7,8},{8,9},{9,10},{10,1... | collective-permute-start | bytes 49160 | tf_op jit(solution)/shard_map/ppermute | solution.py:29
  59.7 8.3 %collective-permute-start.2 = (f32[1,16,256]{2,1,0:T(8,128)}, f32[1,16,256]{2,1,0:T(8,128)}, u32[]{:S(2)}, u32[]{:S(2)}) collective-permute-start(f32[1,16,256]{2,1,0:T(8,128)} %collective-permute-done.1), channel_id=1, source_target_pairs={{0,1},{1,2},{2,3},{3,4},{4,5},{5,6},{6,7},{7,8},{8,9},{9,10},{10,1... | collective-permute-start | bytes 49160 | tf_op jit(solution)/shard_map/ppermute | solution.py:29
  63.5 24.6 %collective-permute-start.9 = (f32[1,16,256]{2,1,0:T(8,128)}, f32[1,16,256]{2,1,0:T(8,128)S(1)}, u32[]{:S(2)}, u32[]{:S(2)}) collective-permute-start(f32[1,16,256]{2,1,0:T(8,128)} %collective-permute-done.8), channel_id=1, source_target_pairs={{1,0},{2,1},{3,2},{4,3},{5,4},{6,5},{7,6},{8,7},{9,8},{10,9},{11,1... | collective-permute-start | bytes 49160 | tf_op jit(solution)/shard_map/ppermute | solution.py:32
  68.0 21.3 %collective-permute-start.3 = (f32[1,16,256]{2,1,0:T(8,128)}, f32[1,16,256]{2,1,0:T(8,128)S(1)}, u32[]{:S(2)}, u32[]{:S(2)}) collective-permute-start(f32[1,16,256]{2,1,0:T(8,128)} %collective-permute-done.2), channel_id=1, source_target_pairs={{0,1},{1,2},{2,3},{3,4},{4,5},{5,6},{6,7},{7,8},{8,9},{9,10},{10,1... | collective-permute-start | bytes 49160 | tf_op jit(solution)/shard_map/ppermute | solution.py:29
  88.1 2.6 %collective-permute-start.10 = (f32[1,16,256]{2,1,0:T(8,128)S(1)}, f32[1,16,256]{2,1,0:T(8,128)S(1)}, u32[]{:S(2)}, u32[]{:S(2)}) collective-permute-start(f32[1,16,256]{2,1,0:T(8,128)S(1)} %collective-permute-done.9), channel_id=1, source_target_pairs={{1,0},{2,1},{3,2},{4,3},{5,4},{6,5},{7,6},{8,7},{9,8},{10,9},{11,1... | collective-permute-start | bytes 49160 | tf_op jit(solution)/shard_map/ppermute | solution.py:32
  89.3 5.9 %collective-permute-start.4 = (f32[1,16,256]{2,1,0:T(8,128)S(1)}, f32[1,16,256]{2,1,0:T(8,128)S(1)}, u32[]{:S(2)}, u32[]{:S(2)}) collective-permute-start(f32[1,16,256]{2,1,0:T(8,128)S(1)} %collective-permute-done.3), channel_id=1, source_target_pairs={{0,1},{1,2},{2,3},{3,4},{4,5},{5,6},{6,7},{7,8},{8,9},{9,10},{10,1... | collective-permute-start | bytes 49160 | tf_op jit(solution)/shard_map/ppermute | solution.py:29
  90.7 5.9 %collective-permute-start.11 = (f32[1,16,256]{2,1,0:T(8,128)S(1)}, f32[1,16,256]{2,1,0:T(8,128)S(1)}, u32[]{:S(2)}, u32[]{:S(2)}) collective-permute-start(f32[1,16,256]{2,1,0:T(8,128)S(1)} %collective-permute-done.10), channel_id=1, source_target_pairs={{1,0},{2,1},{3,2},{4,3},{5,4},{6,5},{7,6},{8,7},{9,8},{10,9},{11,1... | collective-permute-start | bytes 49160 | tf_op jit(solution)/shard_map/ppermute | solution.py:32
  95.2 5.9 %collective-permute-start.5 = (f32[1,16,256]{2,1,0:T(8,128)S(1)}, f32[1,16,256]{2,1,0:T(8,128)S(1)}, u32[]{:S(2)}, u32[]{:S(2)}) collective-permute-start(f32[1,16,256]{2,1,0:T(8,128)S(1)} %collective-permute-done.4), channel_id=1, source_target_pairs={{0,1},{1,2},{2,3},{3,4},{4,5},{5,6},{6,7},{7,8},{8,9},{9,10},{10,1... | collective-permute-start | bytes 49160 | tf_op jit(solution)/shard_map/ppermute | solution.py:29
  96.6 5.9 %collective-permute-start.12 = (f32[1,16,256]{2,1,0:T(8,128)S(1)}, f32[1,16,256]{2,1,0:T(8,128)S(1)}, u32[]{:S(2)}, u32[]{:S(2)}) collective-permute-start(f32[1,16,256]{2,1,0:T(8,128)S(1)} %collective-permute-done.11), channel_id=1, source_target_pairs={{1,0},{2,1},{3,2},{4,3},{5,4},{6,5},{7,6},{8,7},{9,8},{10,9},{11,1... | collective-permute-start | bytes 49160 | tf_op jit(solution)/shard_map/ppermute | solution.py:32
  101.0 5.9 %collective-permute-start.6 = (f32[1,16,256]{2,1,0:T(8,128)S(1)}, f32[1,16,256]{2,1,0:T(8,128)S(1)}, u32[]{:S(2)}, u32[]{:S(2)}) collective-permute-start(f32[1,16,256]{2,1,0:T(8,128)S(1)} %collective-permute-done.5), channel_id=1, source_target_pairs={{0,1},{1,2},{2,3},{3,4},{4,5},{5,6},{6,7},{7,8},{8,9},{9,10},{10,1... | collective-permute-start | bytes 49160 | tf_op jit(solution)/shard_map/ppermute | solution.py:29
  102.5 17.6 %collective-permute-start.13 = (f32[1,16,256]{2,1,0:T(8,128)S(1)}, f32[1,16,256]{2,1,0:T(8,128)S(1)}, u32[]{:S(2)}, u32[]{:S(2)}) collective-permute-start(f32[1,16,256]{2,1,0:T(8,128)S(1)} %collective-permute-done.12), channel_id=1, source_target_pairs={{1,0},{2,1},{3,2},{4,3},{5,4},{6,5},{7,6},{8,7},{9,8},{10,9},{11,1... | collective-permute-start | bytes 49160 | tf_op jit(solution)/shard_map/ppermute | solution.py:32
  106.9 17.7 %collective-permute-start.7 = (f32[1,16,256]{2,1,0:T(8,128)S(1)}, f32[1,16,256]{2,1,0:T(8,128)}, u32[]{:S(2)}, u32[]{:S(2)}) collective-permute-start(f32[1,16,256]{2,1,0:T(8,128)S(1)} %collective-permute-done.6), channel_id=1, source_target_pairs={{0,1},{1,2},{2,3},{3,4},{4,5},{5,6},{6,7},{7,8},{8,9},{9,10},{10,1... | collective-permute-start | bytes 49160 | tf_op jit(solution)/shard_map/ppermute | solution.py:29
  120.1 17.9 %collective-permute-start.14 = (f32[1,16,256]{2,1,0:T(8,128)S(1)}, f32[1,16,256]{2,1,0:T(8,128)S(1)}, u32[]{:S(2)}, u32[]{:S(2)}) collective-permute-start(f32[1,16,256]{2,1,0:T(8,128)S(1)} %collective-permute-done.13), channel_id=1, source_target_pairs={{1,0},{2,1},{3,2},{4,3},{5,4},{6,5},{7,6},{8,7},{9,8},{10,9},{11,1... | collective-permute-start | bytes 49160 | tf_op jit(solution)/shard_map/ppermute | solution.py:32
  126.5 17.8 %copy-start.18 = (f32[16]{0:T(128)S(1)}, f32[16]{0:T(128)}, u32[]{:S(2)}) copy-start(f32[16]{0:T(128)} %get-tuple-element.19) | copy-start | bytes 196
  126.5 17.8 %copy-start.19 = (f32[16]{0:T(128)S(1)}, f32[16]{0:T(128)}, u32[]{:S(2)}) copy-start(f32[16]{0:T(128)} %get-tuple-element.20) | copy-start | bytes 196
  126.5 17.8 %copy-start.20 = (pred[16]{0:T(512)(128)(4,1)S(1)}, pred[16]{0:T(512)(128)(4,1)}, u32[]{:S(2)}) copy-start(pred[16]{0:T(512)(128)(4,1)} %get-tuple-element.21) | copy-start | bytes 52
  127.1 17.2 %copy-start.21 = (pred[16]{0:T(512)(128)(4,1)S(1)}, pred[16]{0:T(512)(128)(4,1)}, u32[]{:S(2)}) copy-start(pred[16]{0:T(512)(128)(4,1)} %get-tuple-element.22) | copy-start | bytes 52
  140.9 7.5 %copy-start.11 = (f32[64]{0:T(128)S(1)}, f32[64]{0:T(128)}, u32[]{:S(2)}) copy-start(f32[64]{0:T(128)} %iota_subtract_fusion.1) | copy-start | bytes 772
  144.3 5.5 %copy-start = (f32[64,64,256]{1,0,2:T(8,128)S(1)}, f32[64,64,256]{1,0,2:T(8,128)}, u32[]{:S(2)}) copy-start(f32[64,64,256]{1,0,2:T(8,128)} %copy.90) | copy-start | bytes 12582916
  155.3 2.0 %copy-start.14 = (f32[64]{0:T(128)S(1)}, f32[64]{0:T(128)}, u32[]{:S(2)}) copy-start(f32[64]{0:T(128)} %copy-done.12) | copy-start | bytes 772
  155.3 2.0 %copy-start.17 = (f32[16]{0:T(128)S(1)}, f32[16]{0:T(128)}, u32[]{:S(2)}) copy-start(f32[16]{0:T(128)} %copy-done.16) | copy-start | bytes 196
  157.3 1.6 copy-start.2
  168.2 2.7 %copy-start.5 = (bf16[1024,256]{1,0:T(8,128)(2,1)S(1)}, bf16[1024,256]{1,0:T(8,128)(2,1)}, u32[]{:S(2)}) copy-start(bf16[1024,256]{1,0:T(8,128)(2,1)} %copy-done.4) | copy-start | bytes 1572868
  168.2 2.7 %copy-start.6 = (f32[16,64,256]{2,1,0:T(8,128)S(1)}, f32[16,64,256]{2,1,0:T(8,128)}, u32[]{:S(2)}) copy-start(f32[16,64,256]{2,1,0:T(8,128)} %copy.117) | copy-start | bytes 3145732
  168.2 2.7 %copy-start.7 = (bf16[1024,256]{1,0:T(8,128)(2,1)S(1)}, bf16[1024,256]{1,0:T(8,128)(2,1)}, u32[]{:S(2)}) copy-start(bf16[1024,256]{1,0:T(8,128)(2,1)} %param.9) | copy-start | bytes 1572868
  168.2 2.7 %copy-start.15 = (f32[256]{0:T(256)S(1)}, f32[256]{0:T(256)}, u32[]{:S(2)}) copy-start(f32[256]{0:T(256)} %param.13) | copy-start | bytes 3076
